TPU v7x, 32 devices: a whole 2x2x4 slice. The times are simulated.
32 devices in a mesh: scene: 2 (over y), tok: 4 (over z), col: 2 (over x), rep: 2 (over core).
Axes of the slice: x: 2, y: 2, z: 4, core: 2. Of those that a mesh axis runs over, the one named last changes fastest.
Arguments:
- tokens: float32 [8192, 512], P(('scene', 'tok'), ('col', 'rep')), parts along dimension 0
- w_qkv: float32 [2, 3, 512, 512], P(None, None, None, ('col', 'rep'))
- w_out: float32 [2, 512, 512], P(None, ('col', 'rep')), may hold values from -0.25 to 0.25
- w_up: float32 [2, 512, 2048], P(None, None, ('col', 'rep')), may hold values from -0.25 to 0.25
- w_down: float32 [2, 2048, 512], P(None, ('col', 'rep')), may hold values from -0.125 to 0.125
- attn_gain: float32 [2, 512], replicated, may hold values from 0.1 to 1.9
- mlp_gain: float32 [2, 512], replicated, may hold values from 0.1 to 1.9
- dest_device: int32 [128], P(('scene', 'tok')), parts along dimension 0, may hold values from 0 to 3, as said below
- dest_slot: int32 [128], P(('scene', 'tok')), parts along dimension 0, may hold values from 0 to 15, as said below
- pillar: int32 [8192], P(('scene', 'tok')), parts along dimension 0, may hold values from -1 to 2047, as said below
- depth_weight: float32 [2, 3, 3, 512], replicated, may hold values from -2 to 2
- point_weight: float32 [2, 512, 1024], replicated, may hold values from -0.25 to 0.25
- raster_gain: float32 [2, 512], replicated, may hold values from 0.1 to 1.9
Outputs:
- raster: float32 [128, 32, 512], P(('scene', 'tok', 'rep'), 'col'), parts along dimension 0
There are 2 independent parts, one for each index of `scene`. A program takes and returns all parts, laid end to end along the dimension named above; an argument that names none is the same for every part. Nothing has to cross between parts.
Inputs may be any that keep to these rules, and one draw needn't show every extreme that they name: `dest_device`: together with dest_slot the blocks fill every index of tok's 16 slots exactly once. At most 5 blocks of one index of tok go to one index, and every index sends exactly 5 blocks to some index. `dest_slot`: the slot of the block among the 16 of its destination. The token at Hilbert position t has a cell in raster rows i * 16 to (i + 1) * 16 - 1 with i = t // 1024, or -1 if it has no pillar; several tokens may share a cell.
All inputs are finite; a program needn't handle non-finite values.
Results may differ from a plain program's by a relative error of at most 0.00012.
Values sent between devices are 32-bit elements; how exact they have to be, the bound alone decides.
A program may use at most 128 MiB of HBM per device.

v0:
```python
import functools
import math

import jax
import jax.numpy as jnp
from jax import lax
from jax.experimental import pallas as pl
from jax.experimental.pallas import tpu as pltpu
from jax.sharding import PartitionSpec as P

PATCH = 1024
TR = 16
TC = 16
HD = 16


MATMUL_PRECISION = lax.Precision.HIGH
EPSILON = 1e-05


def layer_norm(values, gain_row):
    average = jnp.mean(values, axis=-1, keepdims=True)
    centered = values - average
    variance = jnp.mean(centered * centered, axis=-1, keepdims=True)
    return centered * lax.rsqrt(variance + EPSILON) * gain_row


def split(values):
    high = values.astype(jnp.bfloat16)
    return high, (values - high.astype(jnp.float32)).astype(jnp.bfloat16)


def bdot(left, right, dims=(((1,), (0,)), ((), ()))):
    return lax.dot_general(left, right, dims, preferred_element_type=jnp.float32)


def dot3(left, right):
    lh, ll = left
    rh, rl = right
    return bdot(lh, rh) + bdot(lh, rl) + bdot(ll, rh)


def attention_kernel(x_ref, gain_ref, w_ref, out_ref, q_s, k_s, v_s):
    cols = w_ref.shape[-1]
    heads = cols // HD
    rows = x_ref.shape[1]
    chunk = 256
    lanes = q_s.shape[-1]

    r = lax.broadcasted_iota(jnp.int32, (cols, lanes), 0)
    c = lax.broadcasted_iota(jnp.int32, (cols, lanes), 1)
    lane = lax.broadcasted_iota(jnp.int32, (1, cols), 1)
    w = [split(w_ref[j]) for j in range(3)]
    for i in range(rows // chunk):
        at = pl.ds(i * chunk, chunk)
        stream = jnp.concatenate([x_ref[j, at, :] for j in range(x_ref.shape[0])], axis=-1)
        normed = split(layer_norm(stream, gain_ref[...]))
        qh, ql = split(dot3(normed, w[0]) * (HD ** (-0.5) * math.log2(math.e)))
        kh, kl = split(dot3(normed, w[1]))
        vh, vl = split(dot3(normed, w[2]))
        for h in range(heads):
            part = c // HD
            inside = (r // HD == h) & (r % HD == c % HD)
            first = (inside & ((part == 0) | (part == 1))).astype(jnp.bfloat16)
            third = (inside & (part == 2)).astype(jnp.bfloat16)
            outer = (inside & ((part == 0) | (part == 2))).astype(jnp.bfloat16)
            middle = (inside & (part == 1)).astype(jnp.bfloat16)
            q_s[h, at, :] = (bdot(qh, first) + bdot(ql, third)).astype(jnp.bfloat16)
            k_s[h, at, :] = (bdot(kh, outer) + bdot(kl, middle)).astype(jnp.bfloat16)
            own = lane // HD == h
            v_s[h, at, :cols] = jnp.where(own, vh.astype(jnp.float32), 0.0).astype(jnp.bfloat16)
            v_s[h, at, cols:] = jnp.where(own, vl.astype(jnp.float32), 1.0).astype(jnp.bfloat16)

    out_ref[...] = jnp.zeros_like(out_ref)
    for i in range(rows // chunk):
        at = pl.ds(i * chunk, chunk)

        def one_head(h, carry):
            scores = bdot(q_s[h, at, :], k_s[h], (((1,), (1,)), ((), ())))
            weights = jnp.exp2(scores - jnp.max(scores, axis=-1, keepdims=True))
            wh, wl = split(weights)
            sums = bdot(wh, v_s[h]) + bdot(wl, v_s[h])
            top, low = sums[:, :cols], sums[:, cols:]
            own = lane // HD == h
            total = jnp.max(jnp.where(own, 0.0, low), axis=-1, keepdims=True)
            out_ref[at, :] += jnp.where(own, (top + low) / total, 0.0)
            return carry

        lax.fori_loop(0, heads, one_head, 0, unroll=2)


def attend(stream, gain_row, weights):
    slots, rows, width = stream.shape
    cols = weights.shape[-1]
    heads = cols // HD
    lanes = max(128, 3 * HD)
    return pl.pallas_call(
        attention_kernel,
        grid=(rows // PATCH,),
        in_specs=[
            pl.BlockSpec((slots, PATCH, width), lambda i: (0, i, 0)),
            pl.BlockSpec((1, slots * width), lambda i: (0, 0)),
            pl.BlockSpec(weights.shape, lambda i: (0, 0, 0)),
        ],
        out_specs=pl.BlockSpec((PATCH, cols), lambda i: (i, 0)),
        out_shape=jax.ShapeDtypeStruct((rows, cols), jnp.float32),
        scratch_shapes=[
            pltpu.VMEM((heads, PATCH, lanes), jnp.bfloat16),
            pltpu.VMEM((heads, PATCH, lanes), jnp.bfloat16),
            pltpu.VMEM((heads, PATCH, 2 * cols), jnp.bfloat16),
        ],
        compiler_params=pltpu.CompilerParams(vmem_limit_bytes=48 * 1024 * 1024),
        name="attend",
    )(stream, gain_row[None, :], weights)


def matmul(left, right):
    return jnp.dot(left, right, precision=MATMUL_PRECISION, preferred_element_type=jnp.float32)


VMEM_LIMIT = 56 * 1024 * 1024
MESH = pl.DeviceIdType.MESH


def position():
    cols, reps = lax.axis_size("col"), lax.axis_size("rep")
    return cols, reps, lax.axis_index("col"), lax.axis_index("rep")


def greet(devices):
    barrier = pltpu.get_barrier_semaphore()
    for device in devices:
        pl.semaphore_signal(barrier, inc=1, device_id=device, device_id_type=MESH)
    pl.semaphore_wait(barrier, len(devices))


def remote(src, dst, send, recv, device):
    return pltpu.make_async_remote_copy(
        src_ref=src, dst_ref=dst, send_sem=send, recv_sem=recv, device_id=device, device_id_type=MESH
    )


def chunks_of(rows):
    pieces = 4 if rows % 64 == 0 else (2 if rows % 16 == 0 else 1)
    return pieces, rows // pieces


def gather_kernel(x_ref, out_ref, xs, xr, fs, fr, ps, pr, local):
    cols, reps, c, r = position()
    rows = x_ref.shape[0]
    pieces, size = chunks_of(rows)
    me = c * reps + r
    mate = {"col": c, "rep": 1 - r}
    others = [{"col": lax.rem(c + d, cols), "rep": r} for d in range(1, cols)]
    greet([mate] + others)
    across, onward = [], []
    for k in range(pieces):
        at = pl.ds(k * size, size)
        for d in range(1, cols):
            copy = remote(
                x_ref.at[at], out_ref.at[me, at], xs.at[d - 1, k], xr.at[d - 1, k], others[d - 1]
            )
            copy.start()
            across.append(copy)
    share = remote(x_ref, out_ref.at[me], ps, pr, mate)
    share.start()
    keep = pltpu.make_async_copy(x_ref, out_ref.at[me], local)
    keep.start()
    for k in range(pieces):
        at = pl.ds(k * size, size)
        for d in range(1, cols):
            across[k * (cols - 1) + d - 1].wait_recv()
            slot = lax.rem(c + cols - d, cols) * reps + r
            copy = remote(
                out_ref.at[slot, at], out_ref.at[slot, at], fs.at[d - 1, k], fr.at[d - 1, k], mate
            )
            copy.start()
            onward.append(copy)
    for copy in across:
        copy.wait_send()
    share.wait()
    keep.wait()
    for copy in onward:
        copy.wait()


def gather(block, collective_id):
    cols, reps = lax.axis_size("col"), lax.axis_size("rep")
    if reps != 2 or cols < 2:
        return lax.all_gather(block, ("col", "rep"), axis=0)
    pieces, _ = chunks_of(block.shape[0])
    dma = pltpu.SemaphoreType.DMA
    return pl.pallas_call(
        gather_kernel,
        out_shape=jax.ShapeDtypeStruct((cols * reps,) + block.shape, block.dtype),
        in_specs=[pl.BlockSpec(memory_space=pltpu.VMEM)],
        out_specs=pl.BlockSpec(memory_space=pltpu.VMEM),
        scratch_shapes=[dma((cols - 1, pieces))] * 4 + [dma, dma, dma],
        compiler_params=pltpu.CompilerParams(
            collective_id=collective_id, has_side_effects=True, vmem_limit_bytes=VMEM_LIMIT
        ),
        name="gather",
    )(block)


def scatter_kernel(p_ref, out_ref, a_ref, s_ref, b_ref, a_s, a_r, b_s, b_r):
    cols, reps, c, r = position()
    rows = p_ref.shape[1]
    pieces, size = chunks_of(rows)
    mate = {"col": c, "rep": 1 - r}
    others = [{"col": lax.rem(c + d, cols), "rep": r} for d in range(1, cols)]
    greet([mate] + others)
    order = [(k, d) for k in range(pieces) for d in range(1, cols)]
    order += [(k, 0) for k in range(pieces)]
    near, far = {}, {}
    for k, d in order:
        at = pl.ds(k * size, size)
        slot = lax.rem(c + d, cols) * reps + 1 - r
        near[k, d] = remote(
            p_ref.at[slot, at], a_ref.at[d, at], a_s.at[d, k], a_r.at[d, k], mate
        )
        near[k, d].start()
    for k, d in order:
        at = pl.ds(k * size, size)
        slot = lax.rem(c + d, cols) * reps + r
        near[k, d].wait_recv()
        total = p_ref[slot, at] + a_ref[d, at]
        if d == 0:
            out_ref[at] = total
        else:
            s_ref[d - 1, at] = total
            far[k, d] = remote(
                s_ref.at[d - 1, at],
                b_ref.at[d - 1, at],
                b_s.at[d - 1, k],
                b_r.at[d - 1, k],
                others[d - 1],
            )
            far[k, d].start()
    for (k, d), copy in far.items():
        at = pl.ds(k * size, size)
        copy.wait_recv()
        out_ref[at] += b_ref[d - 1, at]
    for copy in list(near.values()) + list(far.values()):
        copy.wait_send()


def scatter(parts, collective_id):
    cols, reps = lax.axis_size("col"), lax.axis_size("rep")
    if reps != 2 or cols < 2:
        return lax.psum_scatter(parts, ("col", "rep"), scatter_dimension=0)
    shape, kind = parts.shape[1:], parts.dtype
    pieces, _ = chunks_of(shape[0])
    dma = pltpu.SemaphoreType.DMA
    return pl.pallas_call(
        scatter_kernel,
        out_shape=jax.ShapeDtypeStruct(shape, kind),
        in_specs=[pl.BlockSpec(memory_space=pltpu.VMEM)],
        out_specs=pl.BlockSpec(memory_space=pltpu.VMEM),
        scratch_shapes=[
            pltpu.VMEM((cols,) + shape, kind),
            pltpu.VMEM((cols - 1,) + shape, kind),
            pltpu.VMEM((cols - 1,) + shape, kind),
            dma((cols, pieces)),
            dma((cols, pieces)),
            dma((cols - 1, pieces)),
            dma((cols - 1, pieces)),
        ],
        compiler_params=pltpu.CompilerParams(
            collective_id=collective_id, has_side_effects=True, vmem_limit_bytes=VMEM_LIMIT
        ),
        name="scatter",
    )(parts)


def swap_kernel(p_ref, out_ref, send, recv, local):
    cols, reps, c, r = position()
    me = c * reps + r
    pairs = [(d, e) for d in range(cols - 1, -1, -1) for e in range(reps) if (d, e) != (0, 0)]
    places = [(lax.rem(c + d, cols), lax.rem(r + e, reps)) for d, e in pairs]
    greet([{"col": x, "rep": y} for x, y in places])
    copies = []
    for i, (x, y) in enumerate(places):
        copy = remote(
            p_ref.at[x * reps + y], out_ref.at[me], send.at[i], recv.at[i], {"col": x, "rep": y}
        )
        copy.start()
        copies.append(copy)
    keep = pltpu.make_async_copy(p_ref.at[me], out_ref.at[me], local)
    keep.start()
    keep.wait()
    for copy in copies:
        copy.wait()


def swap(parts, collective_id):
    count = parts.shape[0]
    if count < 2:
        return parts
    dma = pltpu.SemaphoreType.DMA
    return pl.pallas_call(
        swap_kernel,
        out_shape=jax.ShapeDtypeStruct(parts.shape, parts.dtype),
        in_specs=[pl.BlockSpec(memory_space=pltpu.VMEM)],
        out_specs=pl.BlockSpec(memory_space=pltpu.VMEM),
        scratch_shapes=[dma((count - 1,)), dma((count - 1,)), dma],
        compiler_params=pltpu.CompilerParams(
            collective_id=collective_id, has_side_effects=True, vmem_limit_bytes=VMEM_LIMIT
        ),
        name="swap",
    )(parts)


def attention_layer(slots, layer, w_qkv, whole_out, attn_gain, first_id):
    group, rows, width = slots.shape
    attended = attend(slots, attn_gain[layer], w_qkv[layer])
    share = rows // group
    mine = swap(attended.reshape(group, share, attended.shape[1]), first_id)
    mine = mine.transpose(1, 0, 2).reshape(share, -1)
    own = lax.dynamic_slice_in_dim(slots, lax.axis_index(("col", "rep")) * share, share, 1)
    own = own.transpose(1, 0, 2).reshape(share, -1)
    return gather(own + matmul(mine, whole_out[layer]), first_id + 1).reshape(rows, -1)


def mlp_kernel(x_ref, gain_ref, up_ref, down_ref, share, out_ref):
    x = x_ref[...]
    hidden = dot3(split(layer_norm(x, gain_ref[...])), split(up_ref[...]))
    hidden = 0.5 * hidden * (1.0 + lax.erf(hidden * (0.5**0.5)))
    total = dot3(split(hidden), split(down_ref[...])) + x * share
    width = out_ref.shape[-1]
    for j in range(out_ref.shape[0]):
        out_ref[j] = total[:, j * width : (j + 1) * width]


def mlp_partial(stream, layer, w_up, w_down, mlp_gain, slots):
    rows, width = stream.shape
    tile = min(256, rows)
    hidden = w_up.shape[-1]
    group = lax.axis_size("col") * lax.axis_size("rep")

    def kernel(x_ref, gain_ref, up_ref, down_ref, out_ref):
        mlp_kernel(x_ref, gain_ref, up_ref, down_ref, 1.0 / group, out_ref)

    return pl.pallas_call(
        kernel,
        grid=(rows // tile,),
        in_specs=[
            pl.BlockSpec((tile, width), lambda i: (i, 0)),
            pl.BlockSpec((1, width), lambda i: (0, 0)),
            pl.BlockSpec((width, hidden), lambda i: (0, 0)),
            pl.BlockSpec((hidden, width), lambda i: (0, 0)),
        ],
        out_specs=pl.BlockSpec((slots, tile, width // slots), lambda i: (0, i, 0)),
        out_shape=jax.ShapeDtypeStruct((slots, rows, width // slots), jnp.float32),
        compiler_params=pltpu.CompilerParams(vmem_limit_bytes=48 * 1024 * 1024),
        name="mlp",
    )(stream, mlp_gain[layer][None, :], w_up[layer], w_down[layer])


def send_blocks(block_list, dest_device, dest_slot):
    block_count, rows_per_block, feature_width = block_list.shape
    peers = lax.axis_size("tok")
    capacity = max(2, (block_count + peers - 4) // (peers - 1))
    order_index = jnp.arange(block_count, dtype=jnp.int32)
    earlier = (dest_device[:, None] == dest_device[None, :]) & (
        order_index[None, :] < order_index[:, None]
    )
    prior_count = jnp.sum(earlier.astype(jnp.int32), axis=1)
    slot_key = dest_device * capacity + prior_count
    select_entries = (
        jnp.arange(peers * capacity, dtype=jnp.int32)[:, None] == slot_key[None, :]
    ).astype(jnp.float32)
    outgoing = jnp.einsum(
        "jb,brf->jrf", select_entries, block_list, precision=MATMUL_PRECISION
    ).reshape(peers, capacity, rows_per_block, feature_width)
    slot_codes = matmul(select_entries, (dest_slot + 1).astype(jnp.float32)).reshape(
        peers, capacity
    )
    incoming, arrived = (
        lax.all_to_all(outgoing, "tok", split_axis=0, concat_axis=0, tiled=True),
        lax.all_to_all(slot_codes, "tok", split_axis=0, concat_axis=0, tiled=True),
    )
    wanted = (order_index + 1).astype(jnp.float32)
    placing = (wanted[:, None] == arrived.reshape(-1)[None, :]).astype(jnp.float32)
    flat_incoming = incoming.reshape(peers * capacity, rows_per_block, feature_width)
    return jnp.einsum("sj,jrf->srf", placing, flat_incoming, precision=MATMUL_PRECISION)


def raster_cells(extended, depth_weight, point_weight, gain_row):
    row_count = extended.shape[0] - 2
    col_count = extended.shape[1] - 2
    channels = extended.shape[2]
    normed = (
        extended
        * lax.rsqrt(jnp.mean(extended * extended, axis=-1, keepdims=True) + EPSILON)
        * gain_row
    )
    mixed = jnp.zeros((row_count, col_count, channels), jnp.float32)
    for a in range(3):
        for b in range(3):
            mixed = mixed + normed[a : a + row_count, b : b + col_count] * depth_weight[a, b]
    combined = matmul(mixed.reshape(row_count * col_count, channels), point_weight)
    combined = combined.reshape(row_count, col_count, 2 * channels)
    centre = extended[1:-1, 1:-1]
    return centre + combined[..., :channels] * jax.nn.sigmoid(combined[..., channels:])


HALO = 2


def extended_cells(tok, members, rep_rows, full_width):
    cols, reps = members
    tile = []
    for col in range(cols):
        for rep in range(reps):
            y = rep * rep_rows - HALO + jnp.arange(rep_rows + 2 * HALO, dtype=jnp.int32)[:, None]
            x = col * TC - HALO + jnp.arange(TC + 2 * HALO, dtype=jnp.int32)[None, :]
            good = (y >= 0) & (y < TR) & (x >= 0) & (x < full_width)
            tile.append(jnp.where(good, (tok * TR + y) * full_width + x, -2).reshape(-1))
    return jnp.concatenate(tile)


def pool(partial, pillar, cells):
    onehot = (cells[:, None] == pillar[None, :]).astype(jnp.float32)
    return matmul(onehot, partial)


def exchange_rows(tile, ntok, reps):
    count = ntok * reps
    rep = lax.axis_index("rep")
    forward = [(i, i + 1) for i in range(count - 1)]
    backward = [(i + 1, i) for i in range(count - 1)]
    above = lax.ppermute(tile[-2 * HALO : -HALO], ("tok", "rep"), forward)
    below = lax.ppermute(tile[HALO : 2 * HALO], ("tok", "rep"), backward)
    above = jnp.where(rep == 0, above, tile[:HALO])
    below = jnp.where(rep == reps - 1, below, tile[-HALO:])
    return jnp.concatenate([above, tile[HALO:-HALO], below], axis=0)


def on_device(
    tokens,
    w_qkv,
    w_out,
    w_up,
    w_down,
    attn_gain,
    mlp_gain,
    dest_device,
    dest_slot,
    pillar,
    depth_weight,
    point_weight,
    raster_gain,
):
    members = (lax.axis_size("col"), lax.axis_size("rep"))
    group = members[0] * members[1]
    ntok = lax.axis_size("tok")
    whole_out = lax.all_gather(w_out, ("col", "rep"), axis=1, tiled=True)
    slots = gather(tokens, 1)
    stream = attention_layer(slots, 0, w_qkv, whole_out, attn_gain, 2)
    share = scatter(mlp_partial(stream, 0, w_up, w_down, mlp_gain, group), 4)
    width = share.shape[1]
    block_count = dest_device.shape[0]
    block_list = share.reshape(block_count, -1, width)
    moved = send_blocks(block_list, dest_device, dest_slot).reshape(-1, width)
    slots = gather(moved, 5)
    stream = attention_layer(slots, 1, w_qkv, whole_out, attn_gain, 6)
    partial = mlp_partial(stream, 1, w_up, w_down, mlp_gain, 1)[0]

    rep_rows = TR // members[1]
    full_width = TC * members[0]
    cells = extended_cells(lax.axis_index("tok"), members, rep_rows, full_width)
    pooled = pool(partial, pillar, cells)
    tile = scatter(pooled.reshape(group, -1, pooled.shape[1]), 8)
    tile = tile.reshape(rep_rows + 2 * HALO, TC + 2 * HALO, -1)
    tile = exchange_rows(tile, ntok, members[1])
    first = raster_cells(tile, depth_weight[0], point_weight[0], raster_gain[0])
    y = lax.axis_index(("tok", "rep")) * rep_rows - 1 + jnp.arange(rep_rows + 2)[:, None, None]
    x = lax.axis_index("col") * TC - 1 + jnp.arange(TC + 2)[None, :, None]
    inside = (y >= 0) & (y < TR * ntok) & (x >= 0) & (x < full_width)
    first = jnp.where(inside, first, 0.0)
    return raster_cells(first, depth_weight[1], point_weight[1], raster_gain[1])


def solution(mesh):
    placed = (
        P(("scene", "tok"), ("col", "rep")),
        P(None, None, None, ("col", "rep")),
        P(None, ("col", "rep"), None),
        P(None, None, ("col", "rep")),
        P(None, ("col", "rep"), None),
        P(),
        P(),
        P(("scene", "tok")),
        P(("scene", "tok")),
        P(("scene", "tok")),
        P(),
        P(),
        P(),
    )
    return jax.shard_map(
        on_device,
        mesh=mesh,
        in_specs=placed,
        out_specs=P(("scene", "tok", "rep"), "col", None),
        check_vma=False,
    )
```

profile of v0, /device:TPU:1, one launch (start us, length us, event | category | flops | bytes accessed | tf_op | source)
XLA Modules:
  0.0 293.6 jit_solution(12107798142609085074)
XLA Ops:
  10.3 5.4 %all-to-all-start = ((f32[4,1,5]{2,1,0:T(1,128)}), f32[4,1,5]{2,1,0:T(1,128)S(1)}, u32[]{:S(2)}, u32[]{:S(2)}) async-start(f32[4,1,5]{2,1,0:T(1,128)} %bitcast.2), calls=%async_computation | async-start | bytes 4096 | tf_op jit(solution)/shard_map/all_to_all | solution.py:381
  15.7 29.7 %gather.4.x_ref = f32[4,1024,128]{2,1,0:T(8,128)} custom-call(f32[1024,128]{1,0:T(8,128)} %x_ref.1), custom_call_target="tpu_custom_call" | custom-call | tf_op jit(solution)/shard_map/gather/pallas_call | solution.py:193
  47.3 27.6 %attend.2 = f32[1024,128]{1,0:T(8,128)S(1)} custom-call(f32[4,1024,128]{2,1,0:T(8,128)S(1)} %copy-done, f32[1,512]{1,0:T(1,128)S(1)} %get-tuple-element.44.gain_ref, f32[3,512,128]{2,1,0:T(8,128)S(1)} %get-tuple-element.12.w_ref), custom_call_target="tpu_custom_call" | custom-call | tf_op jit(solution)/shard_map/attend/pallas_call | solution.py:97
  75.6 10.0 %swap.2 = f32[4,256,128]{2,1,0:T(8,128)} custom-call(f32[4,256,128]{2,1,0:T(8,128)} %bitcast.96), custom_call_target="tpu_custom_call" | custom-call | tf_op jit(solution)/shard_map/swap/pallas_call | solution.py:301
  85.6 2.1 copy.37
  88.4 3.9 %slice_bitcast_fusion.4 = (f32[512,512]{1,0:T(8,128)S(1)}, f32[512,512]{1,0:T(8,128)}, f32[512,512]{1,0:T(8,128)}, f32[512,512]{1,0:T(8,128)}) fusion(f32[2,512,512]{2,1,0:T(8,128)} %param.17, f32[2,512,512]{2,1,0:T(8,128)} %param.16), kind=kLoop, calls=%fused_computation.16 | loop fusion | bytes 8388608 | tf_op jit(solution)/shard_map/squeeze | solution.py:357
  92.3 3.0 %convolution_add_fusion.1.x_ref = f32[256,512]{1,0:T(8,128)} fusion(f32[256,512]{0,1:T(8,128)} %bitcast.105, f32[2,512,512]{2,1,0:T(8,128)} %all-gather.2.cloned.1.call-done, f32[4,1024,128]{2,1,0:T(8,128)S(1)} %copy-done, s32[]{:T(128)S(6)} %select_n.60), kind=kOutput, calls=%fused_computation.12 | convolution fusion | flops 402784256 | bytes 2621444 | tf_op jit(solution)/shard_map/dot_general | solution.py:118
  95.3 17.7 %gather.5 = f32[4,256,512]{2,1,0:T(8,128)} custom-call(f32[256,512]{1,0:T(8,128)} %convolution_add_fusion.1.x_ref), custom_call_target="tpu_custom_call" | custom-call | tf_op jit(solution)/shard_map/gather/pallas_call | solution.py:193
  113.1 6.6 %mlp.2.p_ref = f32[4,1024,128]{2,1,0:T(8,128)S(1)} custom-call(f32[1024,512]{1,0:T(8,128)} %bitcast.99, f32[1,512]{1,0:T(1,128)S(1)} %get-tuple-element.42.gain_ref, f32[512,512]{1,0:T(8,128)S(1)} %copy-done.5, f32[512,512]{1,0:T(8,128)S(1)} %copy-done.4), custom_call_target="tpu_custom_call" | custom-call | tf_op jit(solution)/shard_map/mlp/pallas_call | solution.py:344
  121.0 17.6 %scatter.2 = f32[1024,128]{1,0:T(8,128)} custom-call(f32[4,1024,128]{2,1,0:T(8,128)} %copy-done.2), custom_call_target="tpu_custom_call" | custom-call | tf_op jit(solution)/shard_map/scatter/pallas_call | solution.py:255
  141.2 4.9 %all-to-all-start.1 = ((f32[4,5,64,128]{3,2,1,0:T(8,128)}), f32[4,5,64,128]{3,2,1,0:T(8,128)S(1)}, u32[]{:S(2)}, u32[]{:S(2)}) async-start(f32[4,5,64,128]{3,2,1,0:T(8,128)} %copy.39), calls=%async_computation.1 | async-start | bytes 1310720 | tf_op jit(solution)/shard_map/all_to_all | solution.py:380
  147.6 15.5 %all-to-all-done.1 = f32[4,5,64,128]{3,2,1,0:T(8,128)S(1)} async-done(((f32[4,5,64,128]{3,2,1,0:T(8,128)}), f32[4,5,64,128]{3,2,1,0:T(8,128)S(1)}, u32[]{:S(2)}, u32[]{:S(2)}) %all-to-all-start.1) | async-done | bytes 655392 | tf_op jit(solution)/shard_map/all_to_all | solution.py:380
  164.6 18.0 %gather.6.x_ref = f32[4,1024,128]{2,1,0:T(8,128)} custom-call(f32[1024,128]{1,0:T(8,128)} %bitcast.102), custom_call_target="tpu_custom_call" | custom-call | tf_op jit(solution)/shard_map/gather/pallas_call | solution.py:193
  184.2 27.5 %attend.3 = f32[1024,128]{1,0:T(8,128)S(1)} custom-call(f32[4,1024,128]{2,1,0:T(8,128)S(1)} %copy-done.1, f32[1,512]{1,0:T(1,128)S(1)} %get-tuple-element.43.gain_ref, f32[3,512,128]{2,1,0:T(8,128)S(1)} %copy-done.6), custom_call_target="tpu_custom_call" | custom-call | tf_op jit(solution)/shard_map/attend/pallas_call | solution.py:97
  212.6 10.0 %swap.3 = f32[4,256,128]{2,1,0:T(8,128)} custom-call(f32[4,256,128]{2,1,0:T(8,128)} %bitcast.97), custom_call_target="tpu_custom_call" | custom-call | tf_op jit(solution)/shard_map/swap/pallas_call | solution.py:301
  222.5 2.0 copy.43
  224.6 2.8 convolution_add_fusion.x_ref
  227.3 17.7 %gather.7 = f32[4,256,512]{2,1,0:T(8,128)} custom-call(f32[256,512]{1,0:T(8,128)} %convolution_add_fusion.x_ref), custom_call_target="tpu_custom_call" | custom-call | tf_op jit(solution)/shard_map/gather/pallas_call | solution.py:193
  245.1 6.5 %mlp.3 = f32[1,1024,512]{2,1,0:T(8,128)S(1)} custom-call(f32[1024,512]{1,0:T(8,128)} %bitcast.98, f32[1,512]{1,0:T(1,128)S(1)} %get-tuple-element.41.gain_ref, f32[512,512]{1,0:T(8,128)S(1)} %copy-done.3, f32[512,512]{1,0:T(8,128)S(1)} %get-tuple-element.7.down_ref), custom_call_target="tpu_custom_call" | custom-call | tf_op jit(solution)/shard_map/mlp/pallas_call | solution.py:344
  251.6 3.5 %fusion.p_ref = f32[4,240,512]{2,1,0:T(8,128)} fusion(f32[1,1024,512]{2,1,0:T(8,128)S(1)} %mlp.3, s32[1024]{0:T(1024)S(1)} %copy-done.16, s32[4,240]{1,0:T(4,128)S(1)} %eq.85), kind=kOutput, calls=%fused_computation | convolution fusion | flops 3020881920 | bytes 4071168 | tf_op jit(solution)/shard_map/dot_general | solution.py:118
  255.1 16.9 %scatter.3 = f32[240,512]{1,0:T(8,128)} custom-call(f32[4,240,512]{2,1,0:T(8,128)} %fusion.p_ref), custom_call_target="tpu_custom_call" | custom-call | tf_op jit(solution)/shard_map/scatter/pallas_call | solution.py:255
  275.2 2.4 collective-permute-start.1
  277.7 3.4 %collective-permute-done.1 = f32[2,20,512]{2,1,0:T(8,128)S(1)} collective-permute-done((f32[2,20,512]{2,1,0:T(8,128)S(1)}, f32[2,20,512]{2,1,0:T(8,128)S(1)}, u32[]{:S(2)}, u32[]{:S(2)}) %collective-permute-start.1) | collective-permute-done | bytes 81952 | tf_op jit(solution)/shard_map/ppermute | solution.py:434
  281.4 3.1 %fusion.4 = f32[10,18,1024]{2,1,0:T(8,128)S(1)} fusion(f32[2,512,1024]{2,1,0:T(8,128)} %param.24, f32[12,20,512]{2,1,0:T(8,128)S(1)} %multiply_multiply_fusion, f32[512]{0:T(512)S(1)} %bitcast.119, f32[512]{0:T(512)S(1)} %bitcast.120, f32[512]{0:T(512)S(1)} %bitcast.121, f32[512]{0:T(512)S(1)} %bitcast.122, f32[512]{0:T(512)S(1)} %bitcast.123, ...), kind=kOutput, calls=%fused_computation.4 | convolution fusion | flops 567797760 | bytes 7276544 | tf_op jit(solution)/shard_map/dot_general | solution.py:118
  (94 shorter events, 21.9 us)
Async XLA Ops:
  6.5 38.8 %copy-start.12 = (f32[2,512]{1,0:T(2,128)S(1)}, f32[2,512]{1,0:T(2,128)}, u32[]{:S(2)}) copy-start(f32[2,512]{1,0:T(2,128)} %param.18) | copy-start | bytes 12292
  6.5 85.8 %all-gather.2.cloned.1.call-start = ((), (), s32[]{:S(2)}) async-start(), calls=%async_computation.2 | async-start | bytes 2621440 | tf_op jit(solution)/shard_map/all_gather | solution.py:458
  10.3 131.0 %all-to-all-start = ((f32[4,1,5]{2,1,0:T(1,128)}), f32[4,1,5]{2,1,0:T(1,128)S(1)}, u32[]{:S(2)}, u32[]{:S(2)}) async-start(f32[4,1,5]{2,1,0:T(1,128)} %bitcast.2), calls=%async_computation | async-start | bytes 4096 | tf_op jit(solution)/shard_map/all_to_all | solution.py:381
  15.7 29.7 %copy-start.10 = (f32[2,3,512,128]{3,2,1,0:T(8,128)S(1)}, f32[2,3,512,128]{3,2,1,0:T(8,128)}, u32[]{:S(2)}) copy-start(f32[2,3,512,128]{3,2,1,0:T(8,128)} %param.14) | copy-start | bytes 4718596
  45.4 1.9 copy-start
  47.3 41.1 %copy-start.13 = (f32[2,512]{1,0:T(2,128)S(1)}, f32[2,512]{1,0:T(2,128)}, u32[]{:S(2)}) copy-start(f32[2,512]{1,0:T(2,128)} %param.19) | copy-start | bytes 12292
  47.3 41.1 %copy-start.14 = (f32[2,512]{1,0:T(2,128)S(1)}, f32[2,512]{1,0:T(2,128)}, u32[]{:S(2)}) copy-start(f32[2,512]{1,0:T(2,128)} %param.25) | copy-start | bytes 12292
  74.8 0.8 copy-start.7
  92.3 20.7 %copy-start.4 = (f32[512,512]{1,0:T(8,128)S(1)}, f32[512,512]{1,0:T(8,128)}, u32[]{:S(2)}) copy-start(f32[512,512]{1,0:T(8,128)} %get-tuple-element.8.down_ref) | copy-start | bytes 3145732
  92.3 20.7 %copy-start.5 = (f32[512,512]{1,0:T(8,128)S(1)}, f32[512,512]{1,0:T(8,128)}, u32[]{:S(2)}) copy-start(f32[512,512]{1,0:T(8,128)} %get-tuple-element.55.up_ref) | copy-start | bytes 3145732
  119.7 1.3 copy-start.2
  138.6 7.6 %copy-start.11 = (f32[2,3,3,512]{3,0,2,1:T(2,128)S(1)}, f32[2,3,3,512]{3,0,2,1:T(2,128)}, u32[]{:S(2)}) copy-start(f32[2,3,3,512]{3,0,2,1:T(2,128)} %param.23) | copy-start | bytes 110596
  141.2 21.8 %all-to-all-start.1 = ((f32[4,5,64,128]{3,2,1,0:T(8,128)}), f32[4,5,64,128]{3,2,1,0:T(8,128)S(1)}, u32[]{:S(2)}, u32[]{:S(2)}) async-start(f32[4,5,64,128]{3,2,1,0:T(8,128)} %copy.39), calls=%async_computation.1 | async-start | bytes 1310720 | tf_op jit(solution)/shard_map/all_to_all | solution.py:380
  163.7 19.0 %copy-start.6 = (f32[3,512,128]{2,1,0:T(8,128)S(1)}, f32[3,512,128]{2,1,0:T(8,128)}, u32[]{:S(2)}) copy-start(f32[3,512,128]{2,1,0:T(8,128)} %get-tuple-element.11.w_ref) | copy-start | bytes 2359300
  182.6 1.6 copy-start.1
  184.2 40.3 %copy-start.9 = (f32[2,512,512]{2,1,0:T(8,128)S(1)}, f32[2,512,512]{2,1,0:T(8,128)}, u32[]{:S(2)}) copy-start(f32[2,512,512]{2,1,0:T(8,128)} %all-gather.2.cloned.1.call-done) | copy-start | bytes 6291460
  211.8 0.8 copy-start.8
  224.6 20.5 %copy-start.3 = (f32[512,512]{1,0:T(8,128)S(1)}, f32[512,512]{1,0:T(8,128)}, u32[]{:S(2)}) copy-start(f32[512,512]{1,0:T(8,128)} %get-tuple-element.56.up_ref) | copy-start | bytes 3145732
  245.1 6.5 %copy-start.16 = (s32[1024]{0:T(1024)S(1)}, s32[1024]{0:T(1024)}, u32[]{:S(2)}) copy-start(s32[1024]{0:T(1024)} %param.22) | copy-start | bytes 12292
  272.0 5.6 %slice-start = ((f32[240,512]{1,0:T(8,128)}), f32[160,512]{1,0:T(8,128)S(1)}, s32[]{:S(2)}) async-start(f32[240,512]{1,0:T(8,128)} %scatter.3), calls=%async_computation.3 | async-start | bytes 655360 | tf_op jit(solution)/shard_map/slice | solution.py:437
  273.1 4.5 %collective-permute-start = (f32[2,20,512]{2,1,0:T(8,128)S(1)}, f32[2,20,512]{2,1,0:T(8,128)S(1)}, u32[]{:S(2)}, u32[]{:S(2)}) collective-permute-start(f32[2,20,512]{2,1,0:T(8,128)S(1)} %slice.223), channel_id=1, source_target_pairs={{0,1},{1,4},{4,5},{5,8},{8,9},{9,12},{12,13},{2,3},{3,6},{6,7},{7,... | collective-permute-start | bytes 245768 | tf_op jit(solution)/shard_map/ppermute | solution.py:433
  275.2 5.9 %collective-permute-start.1 = (f32[2,20,512]{2,1,0:T(8,128)S(1)}, f32[2,20,512]{2,1,0:T(8,128)S(1)}, u32[]{:S(2)}, u32[]{:S(2)}) collective-permute-start(f32[2,20,512]{2,1,0:T(8,128)S(1)} %slice.229), channel_id=1, source_target_pairs={{1,0},{4,1},{5,4},{8,5},{9,8},{12,9},{13,12},{3,2},{6,3},{7,6},{10... | collective-permute-start | bytes 245768 | tf_op jit(solution)/shard_map/ppermute | solution.py:434
  281.4 3.6 %copy-start.15 = (f32[2,512,1024]{2,1,0:T(8,128)S(1)}, f32[2,512,1024]{2,1,0:T(8,128)}, u32[]{:S(2)}) copy-start(f32[2,512,1024]{2,1,0:T(8,128)} %param.24) | copy-start | bytes 12582916
Sparse Core Ops, SparseCore 0:
  8.9 35.4 all-gather.1
where the time goes:
time: 294 us
  Pallas kernels  206 us (70%)
  waiting for transfers between devices  19.6 us (7%)
  local copies, waits for them, and re-layouts  19.2 us (7%)
  matrix products  16.5 us (6%)
  starting transfers between devices  14.7 us (5%)
  between operations  13.9 us (5%)
  other arithmetic  4 us (1%)
    pallas_call x4, Pallas kernels, gather(): pl.pallas_call(gather_kernel, out_shape=jax.ShapeDtypeStruct((cols * reps...  83.1 us
    pallas_call x2, Pallas kernels, attend(): pl.pallas_call(attention_kernel, grid=(rows // PATCH,), in_specs=[pl.Bloc...  55.1 us
    pallas_call x2, Pallas kernels, scatter(): pl.pallas_call(scatter_kernel, out_shape=jax.ShapeDtypeStruct(shape, kind...  34.5 us
    pallas_call x2, Pallas kernels, swap(): pl.pallas_call(swap_kernel, out_shape=jax.ShapeDtypeStruct(parts.shape, p...  19.9 us
    all_to_all x1, waiting for transfers between devices, send_blocks(): lax.all_to_all(outgoing, 'tok', split_axis=0, concat_axis=0, tiled=True)  15.5 us
    dot_general x6, matrix products, matmul(): jnp.dot(left, right, precision=MATMUL_PRECISION, preferred_element_type=j...  14.2 us
    pallas_call x2, Pallas kernels, mlp_partial(): pl.pallas_call(kernel, grid=(rows // tile,), in_specs=[pl.BlockSpec((tile...  13.1 us
  transfers between devices with their start and end apart: 5, of which 2 were waited for; matrix products, arithmetic and copies ran while one was open for 6% of the time, Pallas kernels for 37%

commit v1 on v0

--- a/solution.py
+++ b/solution.py
@@ -40,11 +40,22 @@
     return bdot(lh, rh) + bdot(lh, rl) + bdot(ll, rh)
 
 
-def attention_kernel(x_ref, gain_ref, w_ref, out_ref, q_s, k_s, v_s):
+def attention_kernel(share, source_ref, x_ref, gain_ref, w_ref, o_ref, out_ref, q_s, k_s, v_s, att_s):
     cols = w_ref.shape[-1]
     heads = cols // HD
-    rows = x_ref.shape[1]
-    chunk = 256
+    rows = out_ref.shape[0]
+    chunk = att_s.shape[0]
+    slots, each, block = x_ref.shape[1:4]
+    first_block = pl.program_id(0) * (rows // block)
+
+    def stream_rows(i):
+        parts = []
+        for n in range(chunk // block):
+            at = source_ref[first_block + i * (chunk // block) + n]
+            places = [x_ref[at // each, j, at % each] for j in range(slots)]
+            parts.append(jnp.concatenate(places, axis=-1))
+        return jnp.concatenate(parts, axis=0)
+
     lanes = q_s.shape[-1]
 
     r = lax.broadcasted_iota(jnp.int32, (cols, lanes), 0)
@@ -53,8 +64,7 @@
     w = [split(w_ref[j]) for j in range(3)]
     for i in range(rows // chunk):
         at = pl.ds(i * chunk, chunk)
-        stream = jnp.concatenate([x_ref[j, at, :] for j in range(x_ref.shape[0])], axis=-1)
-        normed = split(layer_norm(stream, gain_ref[...]))
+        normed = split(layer_norm(stream_rows(i), gain_ref[...]))
         qh, ql = split(dot3(normed, w[0]) * (HD ** (-0.5) * math.log2(math.e)))
         kh, kl = split(dot3(normed, w[1]))
         vh, vl = split(dot3(normed, w[2]))
@@ -71,9 +81,10 @@
             v_s[h, at, :cols] = jnp.where(own, vh.astype(jnp.float32), 0.0).astype(jnp.bfloat16)
             v_s[h, at, cols:] = jnp.where(own, vl.astype(jnp.float32), 1.0).astype(jnp.bfloat16)
 
-    out_ref[...] = jnp.zeros_like(out_ref)
+    projection = split(o_ref[...])
     for i in range(rows // chunk):
         at = pl.ds(i * chunk, chunk)
+        att_s[...] = jnp.zeros_like(att_s)
 
         def one_head(h, carry):
             scores = bdot(q_s[h, at, :], k_s[h], (((1,), (1,)), ((), ())))
@@ -83,35 +94,42 @@
             top, low = sums[:, :cols], sums[:, cols:]
             own = lane // HD == h
             total = jnp.max(jnp.where(own, 0.0, low), axis=-1, keepdims=True)
-            out_ref[at, :] += jnp.where(own, (top + low) / total, 0.0)
+            att_s[...] += jnp.where(own, (top + low) / total, 0.0)
             return carry
 
         lax.fori_loop(0, heads, one_head, 0, unroll=2)
-
-
-def attend(stream, gain_row, weights):
-    slots, rows, width = stream.shape
+        out_ref[at, :] = dot3(split(att_s[...]), projection) + stream_rows(i) * share
+
+
+def attend(blocks, source, gain_row, weights, w_out, group):
+    block, width = blocks.shape[3], blocks.shape[1] * blocks.shape[4]
+    rows = source.shape[0] * block
     cols = weights.shape[-1]
     heads = cols // HD
     lanes = max(128, 3 * HD)
     return pl.pallas_call(
-        attention_kernel,
-        grid=(rows // PATCH,),
-        in_specs=[
-            pl.BlockSpec((slots, PATCH, width), lambda i: (0, i, 0)),
-            pl.BlockSpec((1, slots * width), lambda i: (0, 0)),
-            pl.BlockSpec(weights.shape, lambda i: (0, 0, 0)),
-        ],
-        out_specs=pl.BlockSpec((PATCH, cols), lambda i: (i, 0)),
-        out_shape=jax.ShapeDtypeStruct((rows, cols), jnp.float32),
-        scratch_shapes=[
-            pltpu.VMEM((heads, PATCH, lanes), jnp.bfloat16),
-            pltpu.VMEM((heads, PATCH, lanes), jnp.bfloat16),
-            pltpu.VMEM((heads, PATCH, 2 * cols), jnp.bfloat16),
-        ],
+        functools.partial(attention_kernel, 1.0 / group),
+        grid_spec=pltpu.PrefetchScalarGridSpec(
+            num_scalar_prefetch=1,
+            grid=(rows // PATCH,),
+            in_specs=[
+                pl.BlockSpec(blocks.shape, lambda i, source: (0, 0, 0, 0, 0)),
+                pl.BlockSpec((1, width), lambda i, source: (0, 0)),
+                pl.BlockSpec(weights.shape, lambda i, source: (0, 0, 0)),
+                pl.BlockSpec(w_out.shape, lambda i, source: (0, 0)),
+            ],
+            out_specs=pl.BlockSpec((PATCH, width), lambda i, source: (i, 0)),
+            scratch_shapes=[
+                pltpu.VMEM((heads, PATCH, lanes), jnp.bfloat16),
+                pltpu.VMEM((heads, PATCH, lanes), jnp.bfloat16),
+                pltpu.VMEM((heads, PATCH, 2 * cols), jnp.bfloat16),
+                pltpu.VMEM((256, cols), jnp.float32),
+            ],
+        ),
+        out_shape=jax.ShapeDtypeStruct((rows, width), jnp.float32),
         compiler_params=pltpu.CompilerParams(vmem_limit_bytes=48 * 1024 * 1024),
         name="attend",
-    )(stream, gain_row[None, :], weights)
+    )(source, blocks, gain_row[None, :], weights, w_out)
 
 
 def matmul(left, right):
@@ -273,53 +291,202 @@
     )(parts)
 
 
-def swap_kernel(p_ref, out_ref, send, recv, local):
+def total_kernel(
+    p_ref, out_ref, a_ref, s_ref, b_ref, a_s, a_r, b_s, b_r, xs, xr, fs, fr, ps, pr
+):
     cols, reps, c, r = position()
+    rows = p_ref.shape[1]
+    pieces, size = chunks_of(rows)
     me = c * reps + r
-    pairs = [(d, e) for d in range(cols - 1, -1, -1) for e in range(reps) if (d, e) != (0, 0)]
-    places = [(lax.rem(c + d, cols), lax.rem(r + e, reps)) for d, e in pairs]
-    greet([{"col": x, "rep": y} for x, y in places])
-    copies = []
-    for i, (x, y) in enumerate(places):
-        copy = remote(
-            p_ref.at[x * reps + y], out_ref.at[me], send.at[i], recv.at[i], {"col": x, "rep": y}
+    mate = {"col": c, "rep": 1 - r}
+    others = [{"col": lax.rem(c + d, cols), "rep": r} for d in range(1, cols)]
+    greet([mate] + others)
+    order = [(k, d) for k in range(pieces) for d in range(1, cols)]
+    order += [(k, 0) for k in range(pieces)]
+    near, far, across, share, onward = {}, {}, {}, {}, {}
+    for k, d in order:
+        at = pl.ds(k * size, size)
+        slot = lax.rem(c + d, cols) * reps + 1 - r
+        near[k, d] = remote(
+            p_ref.at[slot, at], a_ref.at[d, at], a_s.at[d, k], a_r.at[d, k], mate
         )
-        copy.start()
-        copies.append(copy)
-    keep = pltpu.make_async_copy(p_ref.at[me], out_ref.at[me], local)
-    keep.start()
-    keep.wait()
-    for copy in copies:
-        copy.wait()
-
-
-def swap(parts, collective_id):
-    count = parts.shape[0]
-    if count < 2:
-        return parts
+        near[k, d].start()
+    for k, d in order:
+        if d == 0:
+            continue
+        at = pl.ds(k * size, size)
+        slot = lax.rem(c + d, cols) * reps + r
+        near[k, d].wait_recv()
+        s_ref[d - 1, at] = p_ref[slot, at] + a_ref[d, at]
+        far[k, d] = remote(
+            s_ref.at[d - 1, at], b_ref.at[d - 1, at], b_s.at[d - 1, k], b_r.at[d - 1, k], others[d - 1]
+        )
+        far[k, d].start()
+    for k in range(pieces):
+        at = pl.ds(k * size, size)
+        near[k, 0].wait_recv()
+        total = p_ref[me, at] + a_ref[0, at]
+        for d in range(1, cols):
+            far[k, d].wait_recv()
+            total = total + b_ref[d - 1, at]
+        out_ref[me, at] = total
+        for d in range(1, cols):
+            across[k, d] = remote(
+                out_ref.at[me, at], out_ref.at[me, at], xs.at[d - 1, k], xr.at[d - 1, k], others[d - 1]
+            )
+            across[k, d].start()
+        share[k] = remote(out_ref.at[me, at], out_ref.at[me, at], ps.at[k], pr.at[k], mate)
+        share[k].start()
+    for (k, d), copy in across.items():
+        at = pl.ds(k * size, size)
+        copy.wait_recv()
+        slot = lax.rem(c + cols - d, cols) * reps + r
+        onward[k, d] = remote(
+            out_ref.at[slot, at], out_ref.at[slot, at], fs.at[d - 1, k], fr.at[d - 1, k], mate
+        )
+        onward[k, d].start()
+    for copies in (near, far, across):
+        for copy in copies.values():
+            copy.wait_send()
+    for copies in (share, onward):
+        for copy in copies.values():
+            copy.wait()
+
+
+def total(parts, collective_id):
+    cols, reps = lax.axis_size("col"), lax.axis_size("rep")
+    if reps != 2 or cols < 2:
+        return lax.psum(parts, ("col", "rep"))
+    shape, kind = parts.shape[1:], parts.dtype
+    pieces, _ = chunks_of(shape[0])
     dma = pltpu.SemaphoreType.DMA
     return pl.pallas_call(
-        swap_kernel,
-        out_shape=jax.ShapeDtypeStruct(parts.shape, parts.dtype),
+        total_kernel,
+        out_shape=jax.ShapeDtypeStruct(parts.shape, kind),
         in_specs=[pl.BlockSpec(memory_space=pltpu.VMEM)],
         out_specs=pl.BlockSpec(memory_space=pltpu.VMEM),
-        scratch_shapes=[dma((count - 1,)), dma((count - 1,)), dma],
+        scratch_shapes=[
+            pltpu.VMEM((cols,) + shape, kind),
+            pltpu.VMEM((cols - 1,) + shape, kind),
+            pltpu.VMEM((cols - 1,) + shape, kind),
+            dma((cols, pieces)),
+            dma((cols, pieces)),
+        ]
+        + [dma((cols - 1, pieces))] * 6
+        + [dma((pieces,))] * 2,
         compiler_params=pltpu.CompilerParams(
             collective_id=collective_id, has_side_effects=True, vmem_limit_bytes=VMEM_LIMIT
         ),
-        name="swap",
+        name="total",
     )(parts)
 
 
-def attention_layer(slots, layer, w_qkv, whole_out, attn_gain, first_id):
-    group, rows, width = slots.shape
-    attended = attend(slots, attn_gain[layer], w_qkv[layer])
-    share = rows // group
-    mine = swap(attended.reshape(group, share, attended.shape[1]), first_id)
-    mine = mine.transpose(1, 0, 2).reshape(share, -1)
-    own = lax.dynamic_slice_in_dim(slots, lax.axis_index(("col", "rep")) * share, share, 1)
-    own = own.transpose(1, 0, 2).reshape(share, -1)
-    return gather(own + matmul(mine, whole_out[layer]), first_id + 1).reshape(rows, -1)
+def move_kernel(o_ref, code_ref, out_ref, arrived_ref, zs, zr, cs, cr, xs, xr, fs, fr, ps, pr, local):
+    cols, reps, c, r = position()
+    ntok, t = lax.axis_size("tok"), lax.axis_index("tok")
+    me = c * reps + r
+    mate = {"col": c, "rep": 1 - r}
+    others = [{"col": lax.rem(c + d, cols), "rep": r} for d in range(1, cols)]
+    peers = [{"tok": lax.rem(t + e, ntok)} for e in range(1, ntok)]
+    greet([mate] + others + peers)
+    along, codes, across, share, onward = [], [], {}, [], []
+    for e in range(1, ntok):
+        target = lax.rem(t + e, ntok)
+        copy = remote(o_ref.at[target], out_ref.at[t, me], zs.at[e - 1], zr.at[e - 1], peers[e - 1])
+        copy.start()
+        along.append(copy)
+        copy = remote(
+            code_ref.at[target], arrived_ref.at[t], cs.at[e - 1], cr.at[e - 1], peers[e - 1]
+        )
+        copy.start()
+        codes.append(copy)
+    keep = pltpu.make_async_copy(o_ref.at[t], out_ref.at[t, me], local.at[0])
+    keep.start()
+    keep_code = pltpu.make_async_copy(code_ref.at[t], arrived_ref.at[t], local.at[1])
+    keep_code.start()
+
+    def hand_on(e):
+        u = lax.rem(t + ntok - e, ntok)
+        for d in range(1, cols):
+            across[e, d].wait_recv()
+            slot = lax.rem(c + cols - d, cols) * reps + r
+            copy = remote(
+                out_ref.at[u, slot], out_ref.at[u, slot], fs.at[e, d - 1], fr.at[e, d - 1], mate
+            )
+            copy.start()
+            onward.append(copy)
+
+    for e in range(ntok):
+        u = lax.rem(t + ntok - e, ntok)
+        if e:
+            along[e - 1].wait_recv()
+        origin = out_ref.at[u, me] if e else o_ref.at[t]
+        for d in range(1, cols):
+            across[e, d] = remote(
+                origin, out_ref.at[u, me], xs.at[e, d - 1], xr.at[e, d - 1], others[d - 1]
+            )
+            across[e, d].start()
+        copy = remote(origin, out_ref.at[u, me], ps.at[e], pr.at[e], mate)
+        copy.start()
+        share.append(copy)
+        if e:
+            hand_on(e - 1)
+    hand_on(ntok - 1)
+    keep.wait()
+    keep_code.wait()
+    for copy in along + list(across.values()):
+        copy.wait_send()
+    for copy in codes + share + onward:
+        copy.wait()
+
+
+def move(outgoing, codes, collective_id):
+    cols, reps, ntok = lax.axis_size("col"), lax.axis_size("rep"), lax.axis_size("tok")
+    if reps != 2 or cols < 2 or ntok < 2:
+        incoming = lax.all_to_all(outgoing, "tok", split_axis=0, concat_axis=0, tiled=True)
+        arrived = lax.all_to_all(codes, "tok", split_axis=0, concat_axis=0, tiled=True)
+        return lax.all_gather(incoming, ("col", "rep"), axis=1), arrived
+    dma = pltpu.SemaphoreType.DMA
+    shape = (ntok, cols * reps) + outgoing.shape[1:]
+    return pl.pallas_call(
+        move_kernel,
+        out_shape=(
+            jax.ShapeDtypeStruct(shape, outgoing.dtype),
+            jax.ShapeDtypeStruct(codes.shape, codes.dtype),
+        ),
+        in_specs=[pl.BlockSpec(memory_space=pltpu.VMEM)] * 2,
+        out_specs=[pl.BlockSpec(memory_space=pltpu.VMEM)] * 2,
+        scratch_shapes=[dma((ntok - 1,))] * 4
+        + [dma((ntok, cols - 1))] * 4
+        + [dma((ntok,))] * 2
+        + [dma((2,))],
+        compiler_params=pltpu.CompilerParams(
+            collective_id=collective_id, has_side_effects=True, vmem_limit_bytes=VMEM_LIMIT
+        ),
+        name="move",
+    )(outgoing, codes)
+
+
+def pick_kernel(index_ref, x_ref, out_ref):
+    for j in range(out_ref.shape[0]):
+        out_ref[j] = x_ref[index_ref[j]]
+
+
+def pick(blocks, index):
+    return pl.pallas_call(
+        pick_kernel,
+        out_shape=jax.ShapeDtypeStruct(index.shape + blocks.shape[1:], blocks.dtype),
+        in_specs=[pl.BlockSpec(memory_space=pltpu.SMEM), pl.BlockSpec(memory_space=pltpu.VMEM)],
+        out_specs=pl.BlockSpec(memory_space=pltpu.VMEM),
+        name="pick",
+    )(index, blocks)
+
+
+def attention_layer(blocks, source, layer, w_qkv, w_out, attn_gain, collective_id):
+    group = blocks.shape[1]
+    terms = attend(blocks, source, attn_gain[layer], w_qkv[layer], w_out[layer], group)
+    rows, width = terms.shape
+    return total(terms.reshape(group, rows // group, width), collective_id).reshape(rows, width)
 
 
 def mlp_kernel(x_ref, gain_ref, up_ref, down_ref, share, out_ref):
@@ -357,33 +524,19 @@
     )(stream, mlp_gain[layer][None, :], w_up[layer], w_down[layer])
 
 
-def send_blocks(block_list, dest_device, dest_slot):
-    block_count, rows_per_block, feature_width = block_list.shape
+def routes(dest_device, dest_slot):
+    count = dest_device.shape[0]
     peers = lax.axis_size("tok")
-    capacity = max(2, (block_count + peers - 4) // (peers - 1))
-    order_index = jnp.arange(block_count, dtype=jnp.int32)
-    earlier = (dest_device[:, None] == dest_device[None, :]) & (
-        order_index[None, :] < order_index[:, None]
-    )
-    prior_count = jnp.sum(earlier.astype(jnp.int32), axis=1)
-    slot_key = dest_device * capacity + prior_count
-    select_entries = (
-        jnp.arange(peers * capacity, dtype=jnp.int32)[:, None] == slot_key[None, :]
-    ).astype(jnp.float32)
-    outgoing = jnp.einsum(
-        "jb,brf->jrf", select_entries, block_list, precision=MATMUL_PRECISION
-    ).reshape(peers, capacity, rows_per_block, feature_width)
-    slot_codes = matmul(select_entries, (dest_slot + 1).astype(jnp.float32)).reshape(
-        peers, capacity
-    )
-    incoming, arrived = (
-        lax.all_to_all(outgoing, "tok", split_axis=0, concat_axis=0, tiled=True),
-        lax.all_to_all(slot_codes, "tok", split_axis=0, concat_axis=0, tiled=True),
-    )
-    wanted = (order_index + 1).astype(jnp.float32)
-    placing = (wanted[:, None] == arrived.reshape(-1)[None, :]).astype(jnp.float32)
-    flat_incoming = incoming.reshape(peers * capacity, rows_per_block, feature_width)
-    return jnp.einsum("sj,jrf->srf", placing, flat_incoming, precision=MATMUL_PRECISION)
+    capacity = max(2, (count + peers - 4) // (peers - 1))
+    order = jnp.arange(count, dtype=jnp.int32)
+    earlier = (dest_device[:, None] == dest_device[None, :]) & (order[None, :] < order[:, None])
+    place = dest_device * capacity + jnp.sum(earlier.astype(jnp.int32), axis=1)
+    chosen = jnp.arange(peers * capacity, dtype=jnp.int32)[:, None] == place[None, :]
+    index = jnp.sum(jnp.where(chosen, order[None, :], 0), axis=1)
+    code = jnp.sum(jnp.where(chosen, dest_slot[None, :] + 1, 0), axis=1)
+    code = jnp.pad(code.reshape(peers, capacity), ((0, 0), (0, 128 - capacity)))
+    code = jnp.broadcast_to(code[:, None, :], (peers, 8, 128)).astype(jnp.float32)
+    return index, code, capacity
 
 
 def raster_cells(extended, depth_weight, point_weight, gain_row):
@@ -455,23 +608,28 @@
     members = (lax.axis_size("col"), lax.axis_size("rep"))
     group = members[0] * members[1]
     ntok = lax.axis_size("tok")
-    whole_out = lax.all_gather(w_out, ("col", "rep"), axis=1, tiled=True)
-    slots = gather(tokens, 1)
-    stream = attention_layer(slots, 0, w_qkv, whole_out, attn_gain, 2)
-    share = scatter(mlp_partial(stream, 0, w_up, w_down, mlp_gain, group), 4)
-    width = share.shape[1]
     block_count = dest_device.shape[0]
-    block_list = share.reshape(block_count, -1, width)
-    moved = send_blocks(block_list, dest_device, dest_slot).reshape(-1, width)
-    slots = gather(moved, 5)
-    stream = attention_layer(slots, 1, w_qkv, whole_out, attn_gain, 6)
+    order = jnp.arange(block_count, dtype=jnp.int32)
+    index, codes, capacity = routes(dest_device, dest_slot)
+    width = tokens.shape[1]
+    blocks = gather(tokens, 1).reshape(1, group, block_count, -1, width)
+    stream = attention_layer(blocks, order, 0, w_qkv, w_out, attn_gain, 2)
+    share = scatter(mlp_partial(stream, 0, w_up, w_down, mlp_gain, group), 3)
+    outgoing = pick(share.reshape(block_count, -1, width), index)
+    outgoing = outgoing.reshape(ntok, -1, width)
+    moved, arrived = move(outgoing, codes, 4)
+    blocks = moved.reshape(ntok, group, capacity, -1, width)
+    held = arrived[:, 0, :capacity].reshape(-1).astype(jnp.int32)
+    found = held[None, :] == order[:, None] + 1
+    source = jnp.sum(jnp.where(found, jnp.arange(held.shape[0], dtype=jnp.int32)[None, :], 0), axis=1)
+    stream = attention_layer(blocks, source, 1, w_qkv, w_out, attn_gain, 5)
     partial = mlp_partial(stream, 1, w_up, w_down, mlp_gain, 1)[0]
 
     rep_rows = TR // members[1]
     full_width = TC * members[0]
     cells = extended_cells(lax.axis_index("tok"), members, rep_rows, full_width)
     pooled = pool(partial, pillar, cells)
-    tile = scatter(pooled.reshape(group, -1, pooled.shape[1]), 8)
+    tile = scatter(pooled.reshape(group, -1, pooled.shape[1]), 6)
     tile = tile.reshape(rep_rows + 2 * HALO, TC + 2 * HALO, -1)
     tile = exchange_rows(tile, ntok, members[1])
     first = raster_cells(tile, depth_weight[0], point_weight[0], raster_gain[0])

time: 294 us -> 252 us (0.86)
  waiting for transfers between devices: 19.6 us -> 3.62 us
  between operations: 13.9 us -> 0.56 us
  Pallas kernels: 206 us -> 218 us
  starting transfers between devices: 14.7 us -> 4.75 us
  matrix products: 16.5 us -> 7.68 us
  local copies, waits for them, and re-layouts: 19.2 us -> 11.8 us
    pallas_call x4 -> x6, Pallas kernels: 75 us -> 152 us  [the longest x2 62.2 us: total(): pl.pallas_call(total_kernel, out_shape=jax.ShapeDtypeStruct(parts.shape,...]
    pallas_call x4 -> x1, Pallas kernels: 83.1 us -> 19 us  [gather(): pl.pallas_call(gather_kernel, out_shape=jax.ShapeDtypeStruct((cols * reps...]
    all_to_all x2 -> x0, waiting for transfers between devices: 15.5 us -> none  [the longest x1 15.5 us: send_blocks(): lax.all_to_all(outgoing, 'tok', split_axis=0, concat_axis=0, tiled=True)]
    all_to_all x2 -> x0, starting transfers between devices: 10.3 us -> none  [the longest x1 5.41 us: send_blocks(): lax.all_to_all(slot_codes, 'tok', split_axis=0, concat_axis=0, tiled=True)]
    dot_general x6 -> x3, matrix products: 14.2 us -> 7.68 us  [matmul(): jnp.dot(left, right, precision=MATMUL_PRECISION, preferred_element_type=j...]
    transpose x2 -> x0, local copies, waits for them, and re-layouts: 4.08 us -> none  [attention_layer(): mine = mine.transpose(1, 0, 2).reshape(share, -1)]
    squeeze x1, local copies, waits for them, and re-layouts: 3.92 us -> 0.46 us  [mlp_partial(): w_down[layer]]
    unnamed x35 -> x33, local copies, waits for them, and re-layouts: 5.33 us -> 7.35 us
  transfers between devices with their start and end apart: 5 -> 2, of which waited for: 2 -> 1; matrix products, arithmetic and copies ran while one was open for 6% -> 0% of each run, Pallas kernels for 37% -> 0%
where the time goes in v1:
time: 252 us; the launch traced here: 250 us
  Pallas kernels  218 us (87%)
  local copies, waits for them, and re-layouts  11.8 us (5%)
  matrix products  7.68 us (3%)
  starting transfers between devices  4.75 us (2%)
  waiting for transfers between devices  3.62 us (1%)
  other arithmetic  3.46 us (1%)
    pallas_call x2, Pallas kernels, total(): pl.pallas_call(total_kernel, out_shape=jax.ShapeDtypeStruct(parts.shape,...  62.2 us
    pallas_call x2, Pallas kernels, attend(): pl.pallas_call(functools.partial(attention_kernel, 1.0 / group), grid_spe...  59 us
    pallas_call x2, Pallas kernels, scatter(): pl.pallas_call(scatter_kernel, out_shape=jax.ShapeDtypeStruct(shape, kind...  34.5 us
    pallas_call x1, Pallas kernels, move(): pl.pallas_call(move_kernel, out_shape=(jax.ShapeDtypeStruct(shape, outgoi...  28.4 us
    pallas_call x1, Pallas kernels, gather(): pl.pallas_call(gather_kernel, out_shape=jax.ShapeDtypeStruct((cols * reps...  19 us
    pallas_call x2, Pallas kernels, mlp_partial(): pl.pallas_call(kernel, grid=(rows // tile,), in_specs=[pl.BlockSpec((tile...  13.3 us
    dot_general x3, matrix products, matmul(): jnp.dot(left, right, precision=MATMUL_PRECISION, preferred_element_type=j...  7.68 us
    unnamed x33, local copies, waits for them, and re-layouts  7.35 us
  transfers between devices with their start and end apart: 2, of which 1 were waited for; matrix products, arithmetic and copies ran while one was open for 0% of the time, Pallas kernels for 0%

profile of v1, /device:TPU:1, one launch (start us, length us, event | category | flops | bytes accessed | tf_op | source)
XLA Modules:
  0.0 250.2 jit_solution(1939547889554344147)
XLA Ops:
  0.7 1.5 slice_bitcast_fusion.4
  2.2 19.0 %gather.1 = f32[4,1024,128]{2,1,0:T(8,128)} custom-call(f32[1024,128]{1,0:T(8,128)} %x_ref.1), custom_call_target="tpu_custom_call" | custom-call | tf_op jit(solution)/shard_map/gather/pallas_call | solution.py:211
  21.2 1.6 copy-done
  22.8 29.4 %attend.2 = f32[1024,512]{1,0:T(8,128)S(1)} custom-call(s32[16]{0:T(128)S(1)} %iota.86.source_ref, f32[1,4,16,64,128]{4,3,2,1,0:T(8,128)S(1)} %bitcast.60, f32[1,512]{1,0:T(1,128)S(1)} %get-tuple-element.52.gain_ref, f32[3,512,128]{2,1,0:T(8,128)S(1)} %get-tuple-element.18.w_ref, f32[128,512]{1,0:T(8,128)S(1)} %get-tuple-element.22.o_ref), custom_call_target="tpu_custom_call" | custom-call | tf_op jit(solution)/shard_map/attend/pallas_call | solution.py:110
  52.3 1.3 copy-done.1
  53.6 31.2 %total.2 = f32[4,256,512]{2,1,0:T(8,128)} custom-call(f32[4,256,512]{2,1,0:T(8,128)} %bitcast.61), custom_call_target="tpu_custom_call" | custom-call | tf_op jit(solution)/shard_map/total/pallas_call | solution.py:363
  85.3 6.8 %mlp.2.p_ref = f32[4,1024,128]{2,1,0:T(8,128)S(1)} custom-call(f32[1024,512]{1,0:T(8,128)} %bitcast.64, f32[1,512]{1,0:T(1,128)S(1)} %get-tuple-element.50.gain_ref, f32[512,512]{1,0:T(8,128)S(1)} %get-tuple-element.61.up_ref, f32[512,512]{1,0:T(8,128)S(1)} %get-tuple-element.14.down_ref), custom_call_target="tpu_custom_call" | custom-call | tf_op jit(solution)/shard_map/mlp/pallas_call | solution.py:511
  92.1 1.3 copy-done.2
  93.4 17.6 %scatter.2 = f32[1024,128]{1,0:T(8,128)} custom-call(f32[4,1024,128]{2,1,0:T(8,128)} %copy-done.2), custom_call_target="tpu_custom_call" | custom-call | tf_op jit(solution)/shard_map/scatter/pallas_call | solution.py:273
  111.9 1.9 pick.1
  114.5 28.4 %move.1 = (f32[4,4,320,128]{3,2,1,0:T(8,128)}, f32[4,8,128]{2,1,0:T(8,128)}) custom-call(f32[4,320,128]{2,1,0:T(8,128)} %bitcast.66, f32[4,8,128]{2,1,0:T(8,128)} %broadcast_in_dim.85.code_ref), custom_call_target="tpu_custom_call" | custom-call | tf_op jit(solution)/shard_map/move/pallas_call | solution.py:451
  143.9 1.7 copy-done.4
  145.6 29.6 %attend.3 = f32[1024,512]{1,0:T(8,128)S(1)} custom-call(s32[16]{0:T(128)S(1)} %select_reduce_fusion.source_ref, f32[4,4,5,64,128]{4,3,2,1,0:T(8,128)S(1)} %bitcast.63, f32[1,512]{1,0:T(1,128)S(1)} %get-tuple-element.51.gain_ref, f32[3,512,128]{2,1,0:T(8,128)S(1)} %get-tuple-element.17.w_ref, f32[128,512]{1,0:T(8,128)S(1)} %get-tuple-element.21.o_ref), custom_call_target="tpu_custom_call" | custom-call | tf_op jit(solution)/shard_map/attend/pallas_call | solution.py:110
  175.2 1.3 copy-done.3
  176.5 31.0 %total.3 = f32[4,256,512]{2,1,0:T(8,128)} custom-call(f32[4,256,512]{2,1,0:T(8,128)} %bitcast.62), custom_call_target="tpu_custom_call" | custom-call | tf_op jit(solution)/shard_map/total/pallas_call | solution.py:363
  207.6 6.5 %mlp.3 = f32[1,1024,512]{2,1,0:T(8,128)S(1)} custom-call(f32[1024,512]{1,0:T(8,128)} %bitcast.65, f32[1,512]{1,0:T(1,128)S(1)} %get-tuple-element.49.gain_ref, f32[512,512]{1,0:T(8,128)S(1)} %get-tuple-element.62.up_ref, f32[512,512]{1,0:T(8,128)S(1)} %get-tuple-element.13.down_ref), custom_call_target="tpu_custom_call" | custom-call | tf_op jit(solution)/shard_map/mlp/pallas_call | solution.py:511
  214.1 3.5 %fusion.p_ref = f32[4,240,512]{2,1,0:T(8,128)} fusion(f32[1,1024,512]{2,1,0:T(8,128)S(1)} %mlp.3, s32[1024]{0:T(1024)S(1)} %copy-done.15, s32[4,240]{1,0:T(4,128)S(1)} %eq.66), kind=kOutput, calls=%fused_computation | convolution fusion | flops 3020881920 | bytes 4071168 | tf_op jit(solution)/shard_map/dot_general | solution.py:136
  217.7 16.9 %scatter.3 = f32[240,512]{1,0:T(8,128)} custom-call(f32[4,240,512]{2,1,0:T(8,128)} %fusion.p_ref), custom_call_target="tpu_custom_call" | custom-call | tf_op jit(solution)/shard_map/scatter/pallas_call | solution.py:273
  234.6 1.1 fusion.76
  235.7 2.8 %collective-permute-start = (f32[2,20,512]{2,1,0:T(8,128)S(1)}, f32[2,20,512]{2,1,0:T(8,128)S(1)}, u32[]{:S(2)}, u32[]{:S(2)}) collective-permute-start(f32[2,20,512]{2,1,0:T(8,128)S(1)} %slice.227), channel_id=1, source_target_pairs={{0,1},{1,4},{4,5},{5,8},{8,9},{9,12},{12,13},{2,3},{3,6},{6,7},{7,... | collective-permute-start | bytes 245768 | tf_op jit(solution)/shard_map/ppermute | solution.py:586
  238.6 1.9 collective-permute-start.1
  240.9 3.6 %collective-permute-done.1 = f32[2,20,512]{2,1,0:T(8,128)S(1)} collective-permute-done((f32[2,20,512]{2,1,0:T(8,128)S(1)}, f32[2,20,512]{2,1,0:T(8,128)S(1)}, u32[]{:S(2)}, u32[]{:S(2)}) %collective-permute-start.1) | collective-permute-done | bytes 81952 | tf_op jit(solution)/shard_map/ppermute | solution.py:587
  244.8 3.1 %fusion.4 = f32[10,18,1024]{2,1,0:T(8,128)S(1)} fusion(f32[2,512,1024]{2,1,0:T(8,128)} %param.24, f32[12,20,512]{2,1,0:T(8,128)S(1)} %multiply_multiply_fusion, f32[512]{0:T(512)S(1)} %bitcast.71, f32[512]{0:T(512)S(1)} %bitcast.72, f32[512]{0:T(512)S(1)} %bitcast.73, f32[512]{0:T(512)S(1)} %bitcast.74, f32[512]{0:T(512)S(1)} %bitcast.75, ...), kind=kOutput, calls=%fused_computation.4 | convolution fusion | flops 567797760 | bytes 7276544 | tf_op jit(solution)/shard_map/dot_general | solution.py:136
  248.4 1.0 fusion.2
  (79 shorter events, 5.4 us)
Async XLA Ops:
  0.0 2.2 copy-start.7
  0.7 1.6 copy-start.9
  21.2 1.6 copy-start
  22.8 62.0 %copy-start.10 = (f32[2,512]{1,0:T(2,128)S(1)}, f32[2,512]{1,0:T(2,128)}, u32[]{:S(2)}) copy-start(f32[2,512]{1,0:T(2,128)} %param.19) | copy-start | bytes 12292
  52.3 1.3 copy-start.1
  53.6 31.2 %copy-start.5 = (f32[2,512,512]{2,1,0:T(8,128)S(1)}, f32[2,512,512]{2,1,0:T(8,128)}, u32[]{:S(2)}) copy-start(f32[2,512,512]{2,1,0:T(8,128)} %param.17) | copy-start | bytes 6291460
  53.6 31.2 %copy-start.6 = (f32[2,512,512]{2,1,0:T(8,128)S(1)}, f32[2,512,512]{2,1,0:T(8,128)}, u32[]{:S(2)}) copy-start(f32[2,512,512]{2,1,0:T(8,128)} %param.16) | copy-start | bytes 6291460
  92.1 1.3 copy-start.2
  93.4 17.6 %copy-start.12 = (s32[16]{0:T(128)S(1)}, s32[16]{0:T(128)}, u32[]{:S(2)}) copy-start(s32[16]{0:T(128)} %param.20) | copy-start | bytes 196
  93.4 17.8 %copy-start.13 = (s32[16]{0:T(128)S(1)}, s32[16]{0:T(128)}, u32[]{:S(2)}) copy-start(s32[16]{0:T(128)} %param.21) | copy-start | bytes 196
  143.9 1.7 copy-start.4
  175.2 1.3 copy-start.3
  207.6 6.5 %copy-start.15 = (s32[1024]{0:T(1024)S(1)}, s32[1024]{0:T(1024)}, u32[]{:S(2)}) copy-start(s32[1024]{0:T(1024)} %param.22) | copy-start | bytes 12292
  217.7 22.8 %copy-start.11 = (f32[2,512]{1,0:T(2,128)S(1)}, f32[2,512]{1,0:T(2,128)}, u32[]{:S(2)}) copy-start(f32[2,512]{1,0:T(2,128)} %param.25) | copy-start | bytes 12292
  217.7 22.9 %copy-start.8 = (f32[2,3,3,512]{3,0,2,1:T(2,128)S(1)}, f32[2,3,3,512]{3,0,2,1:T(2,128)}, u32[]{:S(2)}) copy-start(f32[2,3,3,512]{3,0,2,1:T(2,128)} %param.23) | copy-start | bytes 110596
  234.6 6.2 %slice-start = ((f32[240,512]{1,0:T(8,128)}), f32[160,512]{1,0:T(8,128)S(1)}, s32[]{:S(2)}) async-start(f32[240,512]{1,0:T(8,128)} %scatter.3), calls=%async_computation | async-start | bytes 655360 | tf_op jit(solution)/shard_map/slice | solution.py:590
  235.7 5.1 %collective-permute-start = (f32[2,20,512]{2,1,0:T(8,128)S(1)}, f32[2,20,512]{2,1,0:T(8,128)S(1)}, u32[]{:S(2)}, u32[]{:S(2)}) collective-permute-start(f32[2,20,512]{2,1,0:T(8,128)S(1)} %slice.227), channel_id=1, source_target_pairs={{0,1},{1,4},{4,5},{5,8},{8,9},{9,12},{12,13},{2,3},{3,6},{6,7},{7,... | collective-permute-start | bytes 245768 | tf_op jit(solution)/shard_map/ppermute | solution.py:586
  238.6 5.9 %collective-permute-start.1 = (f32[2,20,512]{2,1,0:T(8,128)S(1)}, f32[2,20,512]{2,1,0:T(8,128)S(1)}, u32[]{:S(2)}, u32[]{:S(2)}) collective-permute-start(f32[2,20,512]{2,1,0:T(8,128)S(1)} %slice.233), channel_id=1, source_target_pairs={{1,0},{4,1},{5,4},{8,5},{9,8},{12,9},{13,12},{3,2},{6,3},{7,6},{10... | collective-permute-start | bytes 245768 | tf_op jit(solution)/shard_map/ppermute | solution.py:587
  244.8 3.6 %copy-start.14 = (f32[2,512,1024]{2,1,0:T(8,128)S(1)}, f32[2,512,1024]{2,1,0:T(8,128)}, u32[]{:S(2)}) copy-start(f32[2,512,1024]{2,1,0:T(8,128)} %param.24) | copy-start | bytes 12582916

commit v2 on v1

--- a/solution.py
+++ b/solution.py
@@ -82,8 +82,9 @@
             v_s[h, at, cols:] = jnp.where(own, vl.astype(jnp.float32), 1.0).astype(jnp.bfloat16)
 
     projection = split(o_ref[...])
-    for i in range(rows // chunk):
-        at = pl.ds(i * chunk, chunk)
+
+    def query_rows(i, carry):
+        at = pl.ds(pl.multiple_of(i * chunk, chunk), chunk)
         att_s[...] = jnp.zeros_like(att_s)
 
         def one_head(h, carry):
@@ -97,8 +98,11 @@
             att_s[...] += jnp.where(own, (top + low) / total, 0.0)
             return carry
 
-        lax.fori_loop(0, heads, one_head, 0, unroll=2)
+        lax.fori_loop(0, heads, one_head, 0, unroll=4)
         out_ref[at, :] = dot3(split(att_s[...]), projection) + stream_rows(i) * share
+        return carry
+
+    lax.fori_loop(0, rows // chunk, query_rows, 0)
 
 
 def attend(blocks, source, gain_row, weights, w_out, group):
@@ -159,8 +163,10 @@
 
 
 def chunks_of(rows):
-    pieces = 4 if rows % 64 == 0 else (2 if rows % 16 == 0 else 1)
-    return pieces, rows // pieces
+    for pieces in (8, 5, 4, 2):
+        if rows % (8 * pieces) == 0:
+            return pieces, rows // pieces
+    return 1, rows
 
 
 def gather_kernel(x_ref, out_ref, xs, xr, fs, fr, ps, pr, local):
@@ -221,13 +227,18 @@
     )(block)
 
 
-def scatter_kernel(p_ref, out_ref, a_ref, s_ref, b_ref, a_s, a_r, b_s, b_r):
+def scatter_kernel(edge, p_ref, out_ref, a_ref, s_ref, b_ref, a_s, a_r, b_s, b_r, *halo):
     cols, reps, c, r = position()
     rows = p_ref.shape[1]
     pieces, size = chunks_of(rows)
     mate = {"col": c, "rep": 1 - r}
     others = [{"col": lax.rem(c + d, cols), "rep": r} for d in range(1, cols)]
-    greet([mate] + others)
+    greeted = [mate] + others
+    if edge:
+        ntok, t = lax.axis_size("tok"), lax.axis_index("tok")
+        partner = {"tok": lax.rem(t + jnp.where(r == 0, ntok - 1, 1), ntok), "rep": 1 - r}
+        greeted = greeted + [partner]
+    greet(greeted)
     order = [(k, d) for k in range(pieces) for d in range(1, cols)]
     order += [(k, 0) for k in range(pieces)]
     near, far = {}, {}
@@ -259,11 +270,21 @@
         at = pl.ds(k * size, size)
         copy.wait_recv()
         out_ref[at] += b_ref[d - 1, at]
+    if edge:
+        h_ref, e_ref, h_s, h_r = halo
+        inner = pl.multiple_of(jnp.where(r == 0, edge, rows - 2 * edge), 8)
+        outer = pl.multiple_of(jnp.where(r == 0, 0, rows - edge), 8)
+        e_ref[...] = out_ref[pl.ds(inner, edge)]
+        copy = remote(e_ref, h_ref, h_s, h_r, partner)
+        copy.start()
+        copy.wait()
+        wrapped = jnp.where(r == 0, t == 0, t == ntok - 1)
+        out_ref[pl.ds(outer, edge)] = jnp.where(wrapped, 0.0, h_ref[...])
     for copy in list(near.values()) + list(far.values()):
         copy.wait_send()
 
 
-def scatter(parts, collective_id):
+def scatter(parts, collective_id, edge=0):
     cols, reps = lax.axis_size("col"), lax.axis_size("rep")
     if reps != 2 or cols < 2:
         return lax.psum_scatter(parts, ("col", "rep"), scatter_dimension=0)
@@ -271,7 +292,7 @@
     pieces, _ = chunks_of(shape[0])
     dma = pltpu.SemaphoreType.DMA
     return pl.pallas_call(
-        scatter_kernel,
+        functools.partial(scatter_kernel, edge),
         out_shape=jax.ShapeDtypeStruct(shape, kind),
         in_specs=[pl.BlockSpec(memory_space=pltpu.VMEM)],
         out_specs=pl.BlockSpec(memory_space=pltpu.VMEM),
@@ -283,7 +304,8 @@
             dma((cols, pieces)),
             dma((cols - 1, pieces)),
             dma((cols - 1, pieces)),
-        ],
+        ]
+        + ([pltpu.VMEM((edge, shape[1]), kind)] * 2 + [dma, dma] if edge else []),
         compiler_params=pltpu.CompilerParams(
             collective_id=collective_id, has_side_effects=True, vmem_limit_bytes=VMEM_LIMIT
         ),
@@ -629,9 +651,13 @@
     full_width = TC * members[0]
     cells = extended_cells(lax.axis_index("tok"), members, rep_rows, full_width)
     pooled = pool(partial, pillar, cells)
-    tile = scatter(pooled.reshape(group, -1, pooled.shape[1]), 6)
+    parts = pooled.reshape(group, -1, pooled.shape[1])
+    edge = HALO * (TC + 2 * HALO)
+    inside_kernel = members[0] > 1 and members[1] == 2 and ntok > 1 and edge % 8 == 0
+    tile = scatter(parts, 6, edge if inside_kernel else 0)
     tile = tile.reshape(rep_rows + 2 * HALO, TC + 2 * HALO, -1)
-    tile = exchange_rows(tile, ntok, members[1])
+    if not inside_kernel:
+        tile = exchange_rows(tile, ntok, members[1])
     first = raster_cells(tile, depth_weight[0], point_weight[0], raster_gain[0])
     y = lax.axis_index(("tok", "rep")) * rep_rows - 1 + jnp.arange(rep_rows + 2)[:, None, None]
     x = lax.axis_index("col") * TC - 1 + jnp.arange(TC + 2)[None, :, None]

time: 252 us -> 251 us (level)
  starting transfers between devices: 4.75 us -> 0 us
  waiting for transfers between devices: 3.62 us -> 0 us
  matrix products: 7.68 us -> 10.5 us
    pallas_call x2, Pallas kernels: 34.5 us -> 40.2 us  [scatter(): pl.pallas_call(functools.partial(scatter_kernel, edge), out_shape=jax.Sha...]
    ppermute x2 -> x0, starting transfers between devices: 4.75 us -> none  [the longest x1 2.83 us: exchange_rows(): above = lax.ppermute(tile[-2 * HALO:-HALO], ('tok', 'rep'), forward)]
    pallas_call x2, Pallas kernels: 59 us -> 54.4 us  [attend(): pl.pallas_call(functools.partial(attention_kernel, 1.0 / group), grid_spe...]
    ppermute x2 -> x0, waiting for transfers between devices: 3.62 us -> none  [the longest x1 3.62 us: exchange_rows(): below = lax.ppermute(tile[HALO:2 * HALO], ('tok', 'rep'), backward)]
    dot_general x3, matrix products: 7.68 us -> 10.5 us  [matmul(): jnp.dot(left, right, precision=MATMUL_PRECISION, preferred_element_type=j...]
    unnamed x33 -> x31, local copies, waits for them, and re-layouts: 7.35 us -> 8.68 us
  transfers between devices with their start and end apart: 2 -> 0, of which waited for: 1 -> 0; matrix products, arithmetic and copies ran while one was open for 0% -> 0% of each run, Pallas kernels for 0% -> 0%
where the time goes in v2:
time: 251 us; the launch traced here: 249 us
  Pallas kernels  220 us (88%)
  local copies, waits for them, and re-layouts  11.7 us (5%)
  matrix products  10.5 us (4%)
  other arithmetic  5.95 us (2%)
    pallas_call x2, Pallas kernels, total(): pl.pallas_call(total_kernel, out_shape=jax.ShapeDtypeStruct(parts.shape,...  62.7 us
    pallas_call x2, Pallas kernels, attend(): pl.pallas_call(functools.partial(attention_kernel, 1.0 / group), grid_spe...  54.4 us
    pallas_call x2, Pallas kernels, scatter(): pl.pallas_call(functools.partial(scatter_kernel, edge), out_shape=jax.Sha...  40.2 us
    pallas_call x1, Pallas kernels, move(): pl.pallas_call(move_kernel, out_shape=(jax.ShapeDtypeStruct(shape, outgoi...  28.4 us
    pallas_call x1, Pallas kernels, gather(): pl.pallas_call(gather_kernel, out_shape=jax.ShapeDtypeStruct((cols * reps...  19 us
    pallas_call x2, Pallas kernels, mlp_partial(): pl.pallas_call(kernel, grid=(rows // tile,), in_specs=[pl.BlockSpec((tile...  13.3 us
    dot_general x3, matrix products, matmul(): jnp.dot(left, right, precision=MATMUL_PRECISION, preferred_element_type=j...  10.5 us
    unnamed x31, local copies, waits for them, and re-layouts  8.68 us

profile of v2, /device:TPU:1, one launch (start us, length us, event | category | flops | bytes accessed | tf_op | source)
XLA Modules:
  0.0 248.6 jit_solution(11102338712293790555)
XLA Ops:
  0.0 1.0 convert_reduce_fusion
  2.3 19.0 %gather.1 = f32[4,1024,128]{2,1,0:T(8,128)} custom-call(f32[1024,128]{1,0:T(8,128)} %x_ref.1), custom_call_target="tpu_custom_call" | custom-call | tf_op jit(solution)/shard_map/gather/pallas_call | solution.py:217
  21.4 0.9 copy-done.9
  23.1 27.2 %attend.2 = f32[1024,512]{1,0:T(8,128)S(1)} custom-call(s32[16]{0:T(128)S(1)} %iota.86.source_ref, f32[1,4,16,64,128]{4,3,2,1,0:T(8,128)S(1)} %bitcast.60, f32[1,512]{1,0:T(1,128)S(1)} %get-tuple-element.46.gain_ref, f32[3,512,128]{2,1,0:T(8,128)S(1)} %get-tuple-element.18.w_ref, f32[128,512]{1,0:T(8,128)S(1)} %get-tuple-element.20.o_ref), custom_call_target="tpu_custom_call" | custom-call | tf_op jit(solution)/shard_map/attend/pallas_call | solution.py:114
  50.3 1.3 copy-done.1
  51.6 31.4 %total.2 = f32[4,256,512]{2,1,0:T(8,128)} custom-call(f32[4,256,512]{2,1,0:T(8,128)} %bitcast.61), custom_call_target="tpu_custom_call" | custom-call | tf_op jit(solution)/shard_map/total/pallas_call | solution.py:385
  83.6 6.6 %mlp.2.p_ref = f32[4,1024,128]{2,1,0:T(8,128)S(1)} custom-call(f32[1024,512]{1,0:T(8,128)} %bitcast.64, f32[1,512]{1,0:T(1,128)S(1)} %get-tuple-element.44.gain_ref, f32[512,512]{1,0:T(8,128)S(1)} %get-tuple-element.57.up_ref, f32[512,512]{1,0:T(8,128)S(1)} %get-tuple-element.14.down_ref), custom_call_target="tpu_custom_call" | custom-call | tf_op jit(solution)/shard_map/mlp/pallas_call | solution.py:533
  90.2 1.3 copy-done.2
  91.5 17.8 %scatter.2 = f32[1024,128]{1,0:T(8,128)} custom-call(f32[4,1024,128]{2,1,0:T(8,128)} %copy-done.2), custom_call_target="tpu_custom_call" | custom-call | tf_op jit(solution)/shard_map/scatter/pallas_call | solution.py:294
  109.3 1.9 pick.1
  111.9 28.4 %move.1 = (f32[4,4,320,128]{3,2,1,0:T(8,128)}, f32[4,8,128]{2,1,0:T(8,128)}) custom-call(f32[4,320,128]{2,1,0:T(8,128)} %bitcast.66, f32[4,8,128]{2,1,0:T(8,128)} %broadcast_in_dim.85.code_ref), custom_call_target="tpu_custom_call" | custom-call | tf_op jit(solution)/shard_map/move/pallas_call | solution.py:473
  141.3 1.7 copy-done.4
  143.1 27.2 %attend.3 = f32[1024,512]{1,0:T(8,128)S(1)} custom-call(s32[16]{0:T(128)S(1)} %select_reduce_fusion.source_ref, f32[4,4,5,64,128]{4,3,2,1,0:T(8,128)S(1)} %bitcast.63, f32[1,512]{1,0:T(1,128)S(1)} %get-tuple-element.45.gain_ref, f32[3,512,128]{2,1,0:T(8,128)S(1)} %get-tuple-element.17.w_ref, f32[128,512]{1,0:T(8,128)S(1)} %get-tuple-element.19.o_ref), custom_call_target="tpu_custom_call" | custom-call | tf_op jit(solution)/shard_map/attend/pallas_call | solution.py:114
  170.3 1.3 copy-done.3
  171.6 31.3 %total.3 = f32[4,256,512]{2,1,0:T(8,128)} custom-call(f32[4,256,512]{2,1,0:T(8,128)} %bitcast.62), custom_call_target="tpu_custom_call" | custom-call | tf_op jit(solution)/shard_map/total/pallas_call | solution.py:385
  202.9 6.7 %mlp.3 = f32[1,1024,512]{2,1,0:T(8,128)S(1)} custom-call(f32[1024,512]{1,0:T(8,128)} %bitcast.65, f32[1,512]{1,0:T(1,128)S(1)} %get-tuple-element.43.gain_ref, f32[512,512]{1,0:T(8,128)S(1)} %get-tuple-element.58.up_ref, f32[512,512]{1,0:T(8,128)S(1)} %get-tuple-element.13.down_ref), custom_call_target="tpu_custom_call" | custom-call | tf_op jit(solution)/shard_map/mlp/pallas_call | solution.py:533
  209.6 1.3 copy-done.5
  211.6 5.1 %fusion.p_ref = f32[4,240,512]{2,1,0:T(8,128)} fusion(f32[1,1024,512]{2,1,0:T(8,128)} %copy-done.5, s32[1024]{0:T(1024)S(1)} %copy-done.14, s32[4,240]{1,0:T(4,128)S(1)} %eq.59), kind=kOutput, calls=%fused_computation | convolution fusion | flops 3020881920 | bytes 4071168 | tf_op jit(solution)/shard_map/dot_general | solution.py:140
  216.7 22.5 %scatter.3 = f32[240,512]{1,0:T(8,128)} custom-call(f32[4,240,512]{2,1,0:T(8,128)} %fusion.p_ref), custom_call_target="tpu_custom_call" | custom-call | tf_op jit(solution)/shard_map/scatter/pallas_call | solution.py:294
  239.2 1.1 reshape.275
  240.3 1.1 multiply_reduce_fusion.1
  241.8 3.0 %fusion.4 = f32[10,18,1024]{2,1,0:T(8,128)S(1)} fusion(f32[2,512,1024]{2,1,0:T(8,128)} %param.24, f32[12,20,512]{2,1,0:T(8,128)S(1)} %multiply_multiply_fusion, f32[512]{0:T(512)S(1)} %bitcast.71, f32[512]{0:T(512)S(1)} %bitcast.72, f32[512]{0:T(512)S(1)} %bitcast.73, f32[512]{0:T(512)S(1)} %bitcast.74, f32[512]{0:T(512)S(1)} %bitcast.75, ...), kind=kOutput, calls=%fused_computation.4 | convolution fusion | flops 567797760 | bytes 7276544 | tf_op jit(solution)/shard_map/dot_general | solution.py:140
  245.3 2.5 fusion.2
  247.8 0.8 fusion.37
  (65 shorter events, 5.8 us)
Async XLA Ops:
  0.0 21.3 %copy-start.11 = (f32[2,512]{1,0:T(2,128)S(1)}, f32[2,512]{1,0:T(2,128)}, u32[]{:S(2)}) copy-start(f32[2,512]{1,0:T(2,128)} %param.18) | copy-start | bytes 12292
  0.0 21.3 %copy-start.8 = (f32[2,3,512,128]{3,2,1,0:T(8,128)S(1)}, f32[2,3,512,128]{3,2,1,0:T(8,128)}, u32[]{:S(2)}) copy-start(f32[2,3,512,128]{3,2,1,0:T(8,128)} %param.14) | copy-start | bytes 4718596
  21.3 1.0 copy-start.9
  21.3 1.7 copy-start
  23.1 60.0 %copy-start.12 = (f32[2,512]{1,0:T(2,128)S(1)}, f32[2,512]{1,0:T(2,128)}, u32[]{:S(2)}) copy-start(f32[2,512]{1,0:T(2,128)} %param.19) | copy-start | bytes 12292
  50.3 1.3 copy-start.1
  51.6 31.5 %copy-start.6 = (f32[2,512,512]{2,1,0:T(8,128)S(1)}, f32[2,512,512]{2,1,0:T(8,128)}, u32[]{:S(2)}) copy-start(f32[2,512,512]{2,1,0:T(8,128)} %param.17) | copy-start | bytes 6291460
  51.6 31.5 %copy-start.7 = (f32[2,512,512]{2,1,0:T(8,128)S(1)}, f32[2,512,512]{2,1,0:T(8,128)}, u32[]{:S(2)}) copy-start(f32[2,512,512]{2,1,0:T(8,128)} %param.16) | copy-start | bytes 6291460
  90.2 1.3 copy-start.2
  141.3 1.7 copy-start.4
  170.3 1.3 copy-start.3
  202.9 8.7 %copy-start.14 = (s32[1024]{0:T(1024)S(1)}, s32[1024]{0:T(1024)}, u32[]{:S(2)}) copy-start(s32[1024]{0:T(1024)} %param.22) | copy-start | bytes 12292
  209.6 1.3 copy-start.5
  216.7 23.6 %copy-start.13 = (f32[2,512]{1,0:T(2,128)S(1)}, f32[2,512]{1,0:T(2,128)}, u32[]{:S(2)}) copy-start(f32[2,512]{1,0:T(2,128)} %param.25) | copy-start | bytes 12292
  216.7 25.0 %copy-start.10 = (f32[2,3,3,512]{3,0,2,1:T(2,128)S(1)}, f32[2,3,3,512]{3,0,2,1:T(2,128)}, u32[]{:S(2)}) copy-start(f32[2,3,3,512]{3,0,2,1:T(2,128)} %param.23) | copy-start | bytes 110596
